TPU v7x, 256 devices: a whole 4x4x8 slice. The times are simulated.
256 devices in a mesh: sect: 2 (over core), grp: 16 (over y_hi, z), tp: 8 (over y_lo, x).
Axes of the slice: x: 4, y: 4 (y_hi: 2, y_lo: 2; y = y_hi * 2 + y_lo), z: 8, core: 2. Of those that a mesh axis runs over, the one named last changes fastest.
Arguments:
- queries: bfloat16 [512, 128, 576], P('grp', ('sect', 'tp')), may hold values from -400 to 400, as said below
- latent_cache: bfloat16 [512, 128, 576], P('grp'), may hold values from -6 to 6, as said below
- cache_len: int32 [512], P('grp'), may hold values from 1 to 128, 32768 in all
- value_up: bfloat16 [128, 512, 128], P(('sect', 'tp')), may hold values from -0.25 to 0.25
- out_proj: bfloat16 [16384, 7168], P(('sect', 'tp'), 'grp'), may hold values from -0.046875 to 0.046875
- residual: bfloat16 [512, 7168], P(None, 'grp'), may hold values from -3 to 3
- w_gate: bfloat16 [16, 7168, 2048], P('grp', None, ('sect', 'tp')), may hold values from -0.0625 to 0.0625
- w_up: bfloat16 [16, 7168, 2048], P('grp', None, ('sect', 'tp')), may hold values from -0.0625 to 0.0625
- w_down: bfloat16 [16, 2048, 7168], P('grp', ('sect', 'tp')), may hold values from -0.1875 to 0.1875
- route_ids: int32 [512, 8], replicated, may hold values from 0 to 15, all different within a row; in each aligned block of 512 rows (0 to 511, 512 to 1023, ...) at most 384 rows name the same one
- route_weights: float32 [512, 8], replicated, may hold values from 0.1 to 0.6
Outputs:
- layer_out: bfloat16 [512, 7168], P(('sect', 'tp'), 'grp')
Inputs may be any that keep to these rules, and one draw needn't show every extreme that they name: `queries`: every entry lies in this range. `latent_cache`: every entry lies in this range. `route_ids`: each row names 8 different experts; every expert is named by at most 384 rows, and one expert by exactly 384. `cache_len`: some row has exactly 128 filled positions.
All inputs are finite; a program needn't handle non-finite values. No bound on the sum of `cache_len` on one device may be relied on, other than what follows from the above.
Results may differ from a plain program's by a relative error of at most 0.018.
Values may be sent and summed in bfloat16 or wider, within the bound.
A program may use at most 128 MiB of HBM per device.

v0:
```python
import jax
import jax.numpy as jnp
from jax import lax
from jax.sharding import PartitionSpec as P

LAT = 512
VDIM = 128
TOP = 8
SOFTMAX_SCALE = 0.0721688
MASK_VALUE = -1e30


def slot_tables(route_ids, route_weights, expert_count, capacity):
    row_total = route_ids.shape[0]
    expert_ids = jnp.arange(expert_count, dtype=jnp.int32)
    matches = route_ids[None, :, :] == expert_ids[:, None, None]
    chosen = jnp.any(matches, axis=2)
    weight = jnp.sum(jnp.where(matches, route_weights[None, :, :], 0.0), axis=2)
    slot_rank = jnp.cumsum(chosen.astype(jnp.int32), axis=1) - 1
    slot_ids = jnp.arange(capacity, dtype=jnp.int32)
    placed = chosen[:, :, None] & (slot_rank[:, :, None] == slot_ids[None, None, :])
    row_ids = jnp.arange(row_total, dtype=jnp.int32)
    slot_rows = jnp.sum(jnp.where(placed, row_ids[None, :, None], 0), axis=1)
    slot_valid = jnp.any(placed, axis=1)
    slot_weight = jnp.sum(jnp.where(placed, weight[:, :, None], 0.0), axis=1)
    return (placed, slot_rows, slot_valid, slot_weight)


def pick_slots(source_rows, slot_rows, slot_valid):
    picked = jnp.take(source_rows, slot_rows, axis=0)
    return jnp.where(slot_valid[:, :, None], picked, jnp.zeros_like(picked))


def on_device(
    queries,
    latent_cache,
    cache_len,
    value_up,
    out_proj,
    residual,
    w_gate,
    w_up,
    w_down,
    route_ids,
    route_weights,
):
    local_rows = queries.shape[0]
    local_heads = queries.shape[1]
    scores = (
        jnp.einsum("rhk,rlk->rhl", queries, latent_cache, preferred_element_type=jnp.float32)
        * SOFTMAX_SCALE
    )
    positions = jnp.arange(latent_cache.shape[1], dtype=jnp.int32)
    in_range = positions[None, None, :] < cache_len[:, None, None]
    masked = jnp.where(in_range, scores, MASK_VALUE)
    row_max = jnp.max(masked, axis=2, keepdims=True)
    exp_scores = jnp.where(in_range, jnp.exp(masked - row_max), 0.0)
    probs = (exp_scores / jnp.sum(exp_scores, axis=2, keepdims=True)).astype(jnp.bfloat16)
    latent_out = jnp.einsum(
        "rhl,rlc->rhc", probs, latent_cache[:, :, :LAT], preferred_element_type=jnp.float32
    ).astype(jnp.bfloat16)
    heads_out = jnp.einsum("rhc,hcv->rhv", latent_out, value_up, preferred_element_type=jnp.float32)
    heads_out = heads_out.astype(jnp.bfloat16).reshape(local_rows, local_heads * VDIM)
    partial_attn = jnp.dot(
        lax.all_gather(heads_out, "grp", axis=0, tiled=True),
        out_proj,
        preferred_element_type=jnp.float32,
    )
    row_total = residual.shape[0]
    expert_count = lax.axis_size("grp")
    tensor_count = lax.axis_size(("sect", "tp"))
    tensor_index = lax.axis_index(("sect", "tp"))
    own_expert = lax.axis_index("grp")
    capacity = min(row_total, row_total * TOP * 3 // (2 * expert_count))
    placed, slot_rows, slot_valid, slot_weight = slot_tables(
        route_ids, route_weights, expert_count, capacity
    )
    share_rows = row_total // tensor_count
    attention = lax.psum(partial_attn, ("sect", "tp"))
    layer_input = (residual.astype(jnp.float32) + attention).astype(jnp.bfloat16)
    own_rows = lax.dynamic_slice_in_dim(layer_input, tensor_index * share_rows, share_rows, 0)
    outgoing = pick_slots(layer_input, slot_rows, slot_valid)
    received = lax.all_to_all(outgoing, "grp", split_axis=0, concat_axis=2, tiled=True)
    expert_in = received[0]
    own_weight = lax.dynamic_index_in_dim(slot_weight, own_expert, 0, keepdims=False)
    gate_value = jnp.dot(expert_in, w_gate[0], preferred_element_type=jnp.float32)
    up_value = jnp.dot(expert_in, w_up[0], preferred_element_type=jnp.float32)
    hidden = (own_weight[:, None] * jax.nn.silu(gate_value) * up_value).astype(jnp.bfloat16)
    own_placed = lax.dynamic_index_in_dim(placed, own_expert, 0, keepdims=False).astype(
        jnp.bfloat16
    )
    hidden_rows = jnp.dot(own_placed, hidden, preferred_element_type=jnp.float32).astype(
        jnp.bfloat16
    )
    expert_term = jnp.dot(hidden_rows, w_down[0], preferred_element_type=jnp.float32)
    column_sums = lax.psum_scatter(
        expert_term.astype(jnp.bfloat16), "grp", scatter_dimension=1, tiled=True
    )
    routed_sum = lax.psum_scatter(
        column_sums, ("sect", "tp"), scatter_dimension=0, tiled=True
    ).astype(jnp.float32)
    return (own_rows.astype(jnp.float32) + routed_sum).astype(jnp.bfloat16)


def solution(mesh):
    return jax.shard_map(
        on_device,
        mesh=mesh,
        in_specs=(
            P("grp", ("sect", "tp"), None),
            P("grp", None, None),
            P("grp"),
            P(("sect", "tp"), None, None),
            P(("sect", "tp"), "grp"),
            P(None, "grp"),
            P("grp", None, ("sect", "tp")),
            P("grp", None, ("sect", "tp")),
            P("grp", ("sect", "tp"), None),
            P(),
            P(),
        ),
        out_specs=P(("sect", "tp"), "grp"),
        check_vma=False,
    )
```

profile of v0, /device:TPU:24, one launch (start us, length us, event | category | flops | bytes accessed | tf_op | source)
XLA Modules:
  0.0 729.3 jit_solution(1491521176456997909)
XLA Ops:
  6.5 0.0 copy-start
  6.5 0.0 all-gather.2.cloned.1.call-start
  6.5 0.9 iota_compare_fusion.2
  7.4 0.0 copy-start.1
  7.4 0.0 copy-start.3
  7.4 3.5 fusion.33
  10.9 0.0 copy-start.2
  10.9 3.5 fusion.9
  14.3 0.0 copy-done.1
  14.3 0.4 fusion.22
  14.7 0.6 copy.63
  15.3 0.0 all-gather.2.cloned.1.call-update
  15.4 0.0 all-reduce.2.cloned.1.call-start
  15.4 0.0 copy-done.3
  15.4 0.1 fusion.28
  15.5 1.2 reduce-window.6
  16.7 0.2 slice_reduce_fusion
  16.9 0.1 copy_bitcast_fusion.1
  17.0 3.3 select_reduce_fusion
  20.4 75.0 %all-gather.2.cloned.1.call-done = bf16[512,1024]{1,0:T(8,128)(2,1)} async-done(((bf16[32,1024]{1,0:T(8,128)(2,1)}), bf16[512,1024]{1,0:T(8,128)(2,1)}) %all-gather.2.cloned.1.call-update) | async-done | bytes 1048592 | tf_op jit(solution)/shard_map/all_gather | solution.py:65
  95.4 3.2 fusion.34
  98.6 0.0 all-reduce.2.cloned.1.call-update
  98.6 0.0 copy-done.2
  98.6 0.2 copy.42
  98.8 5.1 fusion.1
  104.0 131.3 %all-reduce.2.cloned.1.call-done = f32[512,448]{1,0:T(8,128)} async-done(((f32[512,448]{1,0:T(8,128)}), f32[512,448]{1,0:T(8,128)}) %all-reduce.2.cloned.1.call-update) | async-done | bytes 917520 | tf_op jit(solution)/shard_map/psum | solution.py:79
  235.3 1.4 add_convert_fusion
  236.7 25.4 %gather_fusion = bf16[6144,448]{1,0:T(8,128)(2,1)} fusion(bf16[512,448]{1,0:T(8,128)(2,1)S(1)} %add_convert_fusion, s32[6144]{0:T(1024)S(1)} %broadcast_clamp_fusion), kind=kCustom, calls=%fused_computation | custom fusion | bytes 11034624 | tf_op jit(solution)/shard_map/jit(_take)/gather | solution.py:30
  262.1 8.3 %copy.49 = bf16[16,384,448]{1,2,0:T(8,128)(2,1)} copy(bf16[16,384,448]{2,1,0:T(8,128)(2,1)} %bitcast.52) | data formatting | bytes 11010048 | tf_op jit(solution)/shard_map/jit(_take)/gather | solution.py:30
  270.5 5.9 select_select_fusion
  276.3 0.0 copy-start.4
  276.3 10.1 %all-to-all-start = ((bf16[16,384,448]{1,2,0:T(8,128)(2,1)}), bf16[16,384,448]{1,2,0:T(8,128)(2,1)}, u32[]{:S(2)}, u32[]{:S(2)}) async-start(bf16[16,384,448]{1,2,0:T(8,128)(2,1)} %select_select_fusion), calls=%async_computation | async-start | bytes 11010048 | tf_op jit(solution)/shard_map/all_to_all | solution.py:83
  286.5 0.0 reduce-scatter.5.cloned.1.call-start
  286.5 0.0 copy-done.4
  286.5 0.1 select_reduce_fusion.2
  286.6 4.6 select_reduce_fusion.1
  291.2 113.3 %all-to-all-done = bf16[16,384,448]{1,2,0:T(8,128)(2,1)} async-done(((bf16[16,384,448]{1,2,0:T(8,128)(2,1)}), bf16[16,384,448]{1,2,0:T(8,128)(2,1)}, u32[]{:S(2)}, u32[]{:S(2)}) %all-to-all-start) | async-done | bytes 5505056 | tf_op jit(solution)/shard_map/all_to_all | solution.py:83
  404.6 0.0 copy-start.5
  404.6 4.9 fusion.7
  409.4 0.0 copy-done.5
  409.4 4.2 fusion.16
  413.7 0.0 copy-done
  413.7 5.4 convolution_convert_fusion
  419.1 0.0 reduce-scatter.5.cloned.1.call-update
  419.2 0.0 reduce-scatter.7.cloned.1.call-start
  419.2 230.0 %reduce-scatter.5.cloned.1.call-done = bf16[512,448]{0,1:T(8,128)(2,1)} async-done(((bf16[512,7168]{0,1:T(8,128)(2,1)}), bf16[512,448]{0,1:T(8,128)(2,1)}) %reduce-scatter.5.cloned.1.call-update) | async-done | bytes 458768 | tf_op jit(solution)/shard_map/reduce_scatter | solution.py:96
  649.3 2.0 copy.52
  651.3 0.0 reduce-scatter.7.cloned.1.call-update
  651.3 70.1 %reduce-scatter.7.cloned.1.call-done = bf16[32,448]{1,0:T(8,128)(2,1)} async-done(((bf16[512,448]{1,0:T(8,128)(2,1)}), bf16[32,448]{1,0:T(8,128)(2,1)}) %reduce-scatter.7.cloned.1.call-update) | async-done | bytes 28688 | tf_op jit(solution)/shard_map/reduce_scatter | solution.py:99
  721.4 1.4 add_convert_fusion.1
  (8 shorter events, 0.1 us)
Async XLA Ops:
  6.5 407.1 %copy-start = (bf16[1,128,7168]{2,1,0:T(8,128)(2,1)S(1)}, bf16[1,128,7168]{2,1,0:T(8,128)(2,1)}, u32[]{:S(2)}) copy-start(bf16[1,128,7168]{2,1,0:T(8,128)(2,1)} %param.19) | copy-start | bytes 5505028
  6.5 88.8 %all-gather.2.cloned.1.call-start = ((), (), s32[]{:S(2)}) async-start(), calls=%async_computation.3 | async-start | bytes 1114112 | tf_op jit(solution)/shard_map/all_gather | solution.py:65
  7.4 6.9 copy-start.1
  7.4 8.0 %copy-start.3 = (s32[512,8]{0,1:T(8,128)S(1)}, s32[512,8]{0,1:T(8,128)}, u32[]{:S(2)}) copy-start(s32[512,8]{0,1:T(8,128)} %param.20) | copy-start | bytes 49156
  10.9 87.7 %copy-start.2 = (bf16[512,448]{0,1:T(8,128)(2,1)S(1)}, bf16[512,448]{0,1:T(8,128)(2,1)}, u32[]{:S(2)}) copy-start(bf16[512,448]{0,1:T(8,128)(2,1)} %param.16) | copy-start | bytes 1376260
  15.4 220.0 %all-reduce.2.cloned.1.call-start = ((), (), s32[]{:S(2)}) async-start(), calls=%async_computation.4 | async-start | bytes 2097152 | tf_op jit(solution)/shard_map/psum | solution.py:79
  276.3 10.2 %copy-start.4 = (f32[512,8]{0,1:T(8,128)S(1)}, f32[512,8]{0,1:T(8,128)}, u32[]{:S(2)}) copy-start(f32[512,8]{0,1:T(8,128)} %param.21) | copy-start | bytes 49156
  276.3 128.2 %all-to-all-start = ((bf16[16,384,448]{1,2,0:T(8,128)(2,1)}), bf16[16,384,448]{1,2,0:T(8,128)(2,1)}, u32[]{:S(2)}, u32[]{:S(2)}) async-start(bf16[16,384,448]{1,2,0:T(8,128)(2,1)} %select_select_fusion), calls=%async_computation | async-start | bytes 11010048 | tf_op jit(solution)/shard_map/all_to_all | solution.py:83
  286.5 362.8 %reduce-scatter.5.cloned.1.call-start = ((), (), s32[]{:S(2)}) async-start(), calls=%async_computation.5 | async-start | bytes 7798784 | tf_op jit(solution)/shard_map/reduce_scatter | solution.py:96
  404.6 4.9 copy-start.5
  419.2 302.3 %reduce-scatter.7.cloned.1.call-start = ((), (), s32[]{:S(2)}) async-start(), calls=%async_computation.6 | async-start | bytes 557056 | tf_op jit(solution)/shard_map/reduce_scatter | solution.py:99
Sparse Core Ops, SparseCore 0:
  15.5 79.8 all-gather.1
  98.7 136.5 all-reduce.1
  419.3 229.9 reduce-scatter.4
  651.6 69.7 reduce-scatter.6
where the time goes:
time: 730 us; the launch traced here: 729 us
  waiting for transfers between devices  620 us (85%)
  local copies, waits for them, and re-layouts  36.9 us (5%)
  matrix products  25 us (3%)
  other arithmetic  24 us (3%)
  between operations  13.3 us (2%)
  starting transfers between devices  10.2 us (1%)
    reduce_scatter x1, waiting for transfers between devices, on_device(): lax.psum_scatter(expert_term.astype(jnp.bfloat16), 'grp', scatter_dimensi...  230 us
    psum x1, waiting for transfers between devices, on_device(): attention = lax.psum(partial_attn, ('sect', 'tp'))  131 us
    all_to_all x1, waiting for transfers between devices, on_device(): lax.all_to_all(outgoing, 'grp', split_axis=0, concat_axis=2, tiled=True)  113 us
    all_gather x1, waiting for transfers between devices, on_device(): lax.all_gather(heads_out, 'grp', axis=0, tiled=True)  75 us
    reduce_scatter x1, waiting for transfers between devices, on_device(): lax.psum_scatter(column_sums, ('sect', 'tp'), scatter_dimension=0, tiled=...  70.1 us
    gather x2, local copies, waits for them, and re-layouts, pick_slots(): picked = jnp.take(source_rows, slot_rows, axis=0)  33.8 us
  transfers between devices with their start and end apart: 5, of which 5 were waited for; matrix products, arithmetic and copies ran while one was open for 2% of the time, Pallas kernels for 0%

commit v1 on v0

--- a/solution.py
+++ b/solution.py
@@ -62,7 +62,9 @@
     heads_out = jnp.einsum("rhc,hcv->rhv", latent_out, value_up, preferred_element_type=jnp.float32)
     heads_out = heads_out.astype(jnp.bfloat16).reshape(local_rows, local_heads * VDIM)
     partial_attn = jnp.dot(
-        lax.all_gather(heads_out, "grp", axis=0, tiled=True),
+        jnp.concatenate(
+            lax.all_to_all(jnp.stack([heads_out] * lax.axis_size("grp")), "grp", 0, 0), axis=0
+        ),
         out_proj,
         preferred_element_type=jnp.float32,
     )

time: 730 us -> 688 us (0.942)
  waiting for transfers between devices: 620 us -> 566 us
  starting transfers between devices: 10.2 us -> 21.7 us
    all_gather x1 -> x0, waiting for transfers between devices: 75 us -> none  [on_device(): lax.all_gather(heads_out, 'grp', axis=0, tiled=True)]
    all_to_all x0 -> x1, waiting for transfers between devices: none -> 20.8 us  [on_device(): lax.all_to_all(jnp.stack([heads_out] * lax.axis_size('grp')), 'grp', 0, 0)]
    all_to_all x0 -> x1, starting transfers between devices: none -> 11.4 us  [on_device(): lax.all_to_all(jnp.stack([heads_out] * lax.axis_size('grp')), 'grp', 0, 0)]
where the time goes in v1:
time: 688 us; the launch traced here: 687 us
  waiting for transfers between devices  566 us (82%)
  local copies, waits for them, and re-layouts  37.4 us (5%)
  matrix products  24.7 us (4%)
  other arithmetic  24 us (3%)
  starting transfers between devices  21.7 us (3%)
  between operations  13.3 us (2%)
    reduce_scatter x1, waiting for transfers between devices, on_device(): lax.psum_scatter(expert_term.astype(jnp.bfloat16), 'grp', scatter_dimensi...  230 us
    psum x1, waiting for transfers between devices, on_device(): attention = lax.psum(partial_attn, ('sect', 'tp'))  132 us
    all_to_all x1, waiting for transfers between devices, on_device(): lax.all_to_all(outgoing, 'grp', split_axis=0, concat_axis=2, tiled=True)  113 us
    reduce_scatter x1, waiting for transfers between devices, on_device(): lax.psum_scatter(column_sums, ('sect', 'tp'), scatter_dimension=0, tiled=...  70.4 us
    gather x2, local copies, waits for them, and re-layouts, pick_slots(): picked = jnp.take(source_rows, slot_rows, axis=0)  33.8 us
    all_to_all x1, waiting for transfers between devices, on_device(): lax.all_to_all(jnp.stack([heads_out] * lax.axis_size('grp')), 'grp', 0, 0)  20.8 us
  transfers between devices with their start and end apart: 5, of which 5 were waited for; matrix products, arithmetic and copies ran while one was open for 2% of the time, Pallas kernels for 0%

profile of v1, /device:TPU:24, one launch (start us, length us, event | category | flops | bytes accessed | tf_op | source)
XLA Modules:
  0.0 687.1 jit_solution(14217199787866913405)
XLA Ops:
  6.5 0.0 copy-start
  6.5 0.9 iota_compare_fusion.2
  7.4 0.0 copy-start.1
  7.4 3.5 fusion.33
  10.9 0.0 copy-start.3
  10.9 3.4 fusion.9
  14.3 0.0 copy-done.1
  14.3 0.0 copy-start.2
  14.3 0.4 fusion.22
  14.7 1.1 stack.3
  15.8 11.4 %all-to-all-start = ((bf16[16,32,1024]{2,1,0:T(8,128)(2,1)}), bf16[16,32,1024]{2,1,0:T(8,128)(2,1)S(1)}, u32[]{:S(2)}, u32[]{:S(2)}) async-start(bf16[16,32,1024]{2,1,0:T(8,128)(2,1)} %stack.3), calls=%async_computation | async-start | bytes 2097152 | tf_op jit(solution)/shard_map/all_to_all | solution.py:66
  27.2 0.0 all-reduce.2.cloned.1.call-start
  27.3 0.0 copy-done.3
  27.3 0.1 fusion.28
  27.4 1.2 reduce-window.6
  28.6 0.2 slice_reduce_fusion
  28.8 0.1 copy_bitcast_fusion.1
  28.9 3.3 select_reduce_fusion
  32.3 20.8 %all-to-all-done = bf16[16,32,1024]{2,1,0:T(8,128)(2,1)S(1)} async-done(((bf16[16,32,1024]{2,1,0:T(8,128)(2,1)}), bf16[16,32,1024]{2,1,0:T(8,128)(2,1)S(1)}, u32[]{:S(2)}, u32[]{:S(2)}) %all-to-all-start) | async-done | bytes 1048608 | tf_op jit(solution)/shard_map/all_to_all | solution.py:66
  53.0 2.9 fusion.34
  56.0 0.0 all-reduce.2.cloned.1.call-update
  56.0 0.0 copy-done.2
  56.0 0.2 copy.42
  56.3 5.1 fusion.1
  61.4 131.6 %all-reduce.2.cloned.1.call-done = f32[512,448]{1,0:T(8,128)} async-done(((f32[512,448]{1,0:T(8,128)}), f32[512,448]{1,0:T(8,128)}) %all-reduce.2.cloned.1.call-update) | async-done | bytes 917520 | tf_op jit(solution)/shard_map/psum | solution.py:81
  193.0 1.4 add_convert_fusion
  194.4 25.4 %gather_fusion = bf16[6144,448]{1,0:T(8,128)(2,1)} fusion(bf16[512,448]{1,0:T(8,128)(2,1)S(1)} %add_convert_fusion, s32[6144]{0:T(1024)S(1)} %broadcast_clamp_fusion), kind=kCustom, calls=%fused_computation | custom fusion | bytes 11034624 | tf_op jit(solution)/shard_map/jit(_take)/gather | solution.py:30
  219.8 8.3 %copy.49 = bf16[16,384,448]{1,2,0:T(8,128)(2,1)} copy(bf16[16,384,448]{2,1,0:T(8,128)(2,1)} %bitcast.53) | data formatting | bytes 11010048 | tf_op jit(solution)/shard_map/jit(_take)/gather | solution.py:30
  228.2 5.9 select_select_fusion
  234.0 0.0 copy-start.4
  234.0 10.1 %all-to-all-start.1 = ((bf16[16,384,448]{1,2,0:T(8,128)(2,1)}), bf16[16,384,448]{1,2,0:T(8,128)(2,1)}, u32[]{:S(2)}, u32[]{:S(2)}) async-start(bf16[16,384,448]{1,2,0:T(8,128)(2,1)} %select_select_fusion), calls=%async_computation.1 | async-start | bytes 11010048 | tf_op jit(solution)/shard_map/all_to_all | solution.py:85
  244.1 0.0 reduce-scatter.5.cloned.1.call-start
  244.2 0.0 copy-done.4
  244.2 0.1 select_reduce_fusion.2
  244.3 4.6 select_reduce_fusion.1
  248.9 113.3 %all-to-all-done.1 = bf16[16,384,448]{1,2,0:T(8,128)(2,1)} async-done(((bf16[16,384,448]{1,2,0:T(8,128)(2,1)}), bf16[16,384,448]{1,2,0:T(8,128)(2,1)}, u32[]{:S(2)}, u32[]{:S(2)}) %all-to-all-start.1) | async-done | bytes 5505056 | tf_op jit(solution)/shard_map/all_to_all | solution.py:85
  362.2 0.0 copy-start.5
  362.2 4.9 fusion.7
  367.1 0.0 copy-done.5
  367.1 4.2 fusion.16
  371.4 0.0 copy-done
  371.4 5.5 convolution_convert_fusion
  376.8 0.0 reduce-scatter.5.cloned.1.call-update
  376.8 0.0 reduce-scatter.7.cloned.1.call-start
  376.9 229.9 %reduce-scatter.5.cloned.1.call-done = bf16[512,448]{0,1:T(8,128)(2,1)} async-done(((bf16[512,7168]{0,1:T(8,128)(2,1)}), bf16[512,448]{0,1:T(8,128)(2,1)}) %reduce-scatter.5.cloned.1.call-update) | async-done | bytes 458768 | tf_op jit(solution)/shard_map/reduce_scatter | solution.py:98
  606.8 2.0 copy.52
  608.8 0.0 reduce-scatter.7.cloned.1.call-update
  608.8 70.4 %reduce-scatter.7.cloned.1.call-done = bf16[32,448]{1,0:T(8,128)(2,1)} async-done(((bf16[512,448]{1,0:T(8,128)(2,1)}), bf16[32,448]{1,0:T(8,128)(2,1)}) %reduce-scatter.7.cloned.1.call-update) | async-done | bytes 28688 | tf_op jit(solution)/shard_map/reduce_scatter | solution.py:101
  679.2 1.4 add_convert_fusion.1
  (9 shorter events, 0.1 us)
Async XLA Ops:
  6.5 364.8 %copy-start = (bf16[1,128,7168]{2,1,0:T(8,128)(2,1)S(1)}, bf16[1,128,7168]{2,1,0:T(8,128)(2,1)}, u32[]{:S(2)}) copy-start(bf16[1,128,7168]{2,1,0:T(8,128)(2,1)} %param.19) | copy-start | bytes 5505028
  7.4 6.9 %copy-start.1 = (bf16[8,512,128]{2,1,0:T(8,128)(2,1)S(1)}, bf16[8,512,128]{2,1,0:T(8,128)(2,1)}, u32[]{:S(2)}) copy-start(bf16[8,512,128]{2,1,0:T(8,128)(2,1)} %param.14) | copy-start | bytes 3145732
  10.9 16.4 %copy-start.3 = (s32[512,8]{0,1:T(8,128)S(1)}, s32[512,8]{0,1:T(8,128)}, u32[]{:S(2)}) copy-start(s32[512,8]{0,1:T(8,128)} %param.20) | copy-start | bytes 49156
  14.3 41.7 %copy-start.2 = (bf16[512,448]{0,1:T(8,128)(2,1)S(1)}, bf16[512,448]{0,1:T(8,128)(2,1)}, u32[]{:S(2)}) copy-start(bf16[512,448]{0,1:T(8,128)(2,1)} %param.16) | copy-start | bytes 1376260
  15.8 37.2 %all-to-all-start = ((bf16[16,32,1024]{2,1,0:T(8,128)(2,1)}), bf16[16,32,1024]{2,1,0:T(8,128)(2,1)S(1)}, u32[]{:S(2)}, u32[]{:S(2)}) async-start(bf16[16,32,1024]{2,1,0:T(8,128)(2,1)} %stack.3), calls=%async_computation | async-start | bytes 2097152 | tf_op jit(solution)/shard_map/all_to_all | solution.py:66
  27.2 165.7 %all-reduce.2.cloned.1.call-start = ((), (), s32[]{:S(2)}) async-start(), calls=%async_computation.4 | async-start | bytes 2097152 | tf_op jit(solution)/shard_map/psum | solution.py:81
  234.0 10.2 %copy-start.4 = (f32[512,8]{0,1:T(8,128)S(1)}, f32[512,8]{0,1:T(8,128)}, u32[]{:S(2)}) copy-start(f32[512,8]{0,1:T(8,128)} %param.21) | copy-start | bytes 49156
  234.0 128.2 %all-to-all-start.1 = ((bf16[16,384,448]{1,2,0:T(8,128)(2,1)}), bf16[16,384,448]{1,2,0:T(8,128)(2,1)}, u32[]{:S(2)}, u32[]{:S(2)}) async-start(bf16[16,384,448]{1,2,0:T(8,128)(2,1)} %select_select_fusion), calls=%async_computation.1 | async-start | bytes 11010048 | tf_op jit(solution)/shard_map/all_to_all | solution.py:85
  244.1 362.6 %reduce-scatter.5.cloned.1.call-start = ((), (), s32[]{:S(2)}) async-start(), calls=%async_computation.5 | async-start | bytes 7798784 | tf_op jit(solution)/shard_map/reduce_scatter | solution.py:98
  362.2 4.9 copy-start.5
  376.8 302.4 %reduce-scatter.7.cloned.1.call-start = ((), (), s32[]{:S(2)}) async-start(), calls=%async_computation.6 | async-start | bytes 557056 | tf_op jit(solution)/shard_map/reduce_scatter | solution.py:101
Sparse Core Ops, SparseCore 0:
  56.1 136.8 all-reduce.1
  377.0 229.7 reduce-scatter.4
  609.3 69.8 reduce-scatter.6
